TPU v7x, 32 devices: a whole 2x2x4 slice. The times are simulated.
32 devices in a mesh: ctx: 16 (over z, y, core), head: 2 (over x).
Axes of the slice: x: 2, y: 2, z: 4, core: 2. Of those that a mesh axis runs over, the one named last changes fastest.
Arguments:
- queries: bfloat16 [4096, 4096], P(('ctx', 'head')), may hold values from -6 to 6
- keys: bfloat16 [4096, 1024], P(('ctx', 'head')), may hold values from -6 to 6
- values: bfloat16 [4096, 1024], P(('ctx', 'head')), may hold values from -6 to 6
- grad_out: bfloat16 [4096, 4096], P(('ctx', 'head')), may hold values from -6 to 6
- doc_ids: int32 [4096], replicated, may hold values from 0 to 3, never falling along the last dimension, each value on 1 to 2048 neighbouring positions
Outputs:
- attended: bfloat16 [4096, 4096], P(('ctx', 'head'))
- grad_queries: bfloat16 [4096, 4096], P(('ctx', 'head'))
- grad_keys: bfloat16 [4096, 1024], P(('ctx', 'head'))
- grad_values: bfloat16 [4096, 1024], P(('ctx', 'head'))
Inputs may be any that keep to these rules, and one draw needn't show every extreme that they name: `doc_ids`: document numbers never fall along the row; every document has 1 to 2048 tokens and one has exactly 2048.
All inputs are finite; a program needn't handle non-finite values.
Results may differ from a plain program's by a relative error of at most 0.023.
Values may be sent and summed in bfloat16 or wider, within the bound.
A program may use at most 64 MiB of HBM per device.

v0:
```python
import functools

import jax
import jax.numpy as jnp
from jax import lax
from jax.experimental import pallas as pl
from jax.experimental.pallas import tpu as pltpu
from jax.sharding import PartitionSpec as P

HD = 128
DOC_MOST = 2048
TILE = 256
LOG2E = 1.4426950408889634
MESH = pl.DeviceIdType.MESH


def place(ctx_low, heads):
    ctx, head = lax.axis_index("ctx"), lax.axis_index("head")
    block = ctx // ctx_low
    me = (ctx - block * ctx_low) * heads + head

    def member(number):
        return (block * ctx_low + number // heads, lax.rem(number, heads))

    return ctx, head, block, me, member


def greet(members, ctx, head, ctx_low, has_prev, has_next):
    barrier = pltpu.get_barrier_semaphore()
    for device in members:
        pl.semaphore_signal(barrier, inc=1, device_id=device, device_id_type=MESH)

    @pl.when(has_prev)
    def _():
        pl.semaphore_signal(barrier, inc=1, device_id=(ctx - ctx_low, head), device_id_type=MESH)

    @pl.when(has_next)
    def _():
        pl.semaphore_signal(barrier, inc=1, device_id=(ctx + ctx_low, head), device_id_type=MESH)

    near = has_prev.astype(jnp.int32) + has_next.astype(jnp.int32)
    pl.semaphore_wait(barrier, len(members) + near)


def fused_kernel(
    heads, ctx_low, blocks, distance, scale,
    start_ref, q_in, k_in, v_in, g_in,
    ao_ref, do_ref, ko_ref, vo_ref,
    qo, go, band, acc, kept, qt, gt, peak, total, ot, dqt, kt, vt, inv, delta,
    att, dq, sums, landed, wide,
    own_sem, send_sem, recv_sem, in_send, in_recv, out_send, out_recv,
):
    group = ctx_low * heads
    rows = q_in.shape[0]
    q_cols = q_in.shape[1] // group
    tokens = qo.shape[0]
    share = q_cols // HD
    factor = scale * LOG2E
    per_block = tokens // TILE
    reach = distance * per_block + 1
    ctx, head, block, me, member = place(ctx_low, heads)
    has_prev, has_next = block > 0, block < blocks - 1
    others = [lax.rem(me + step, group) for step in range(1, group)]
    greet([member(o) for o in others], ctx, head, ctx_low, has_prev, has_next)
    mine = pl.ds(pl.multiple_of(me * rows, rows), rows)
    base = block * tokens
    first_token = base - distance * tokens
    first_kb = jnp.maximum(distance - block, 0) * per_block

    def columns(width, number):
        return pl.ds(pl.multiple_of(number * width, width), width)

    def swap(a, pick_src, pick_dst):
        local = pltpu.make_async_copy(pick_src(me), pick_dst(me), own_sem.at[a])
        local.start()
        line = []
        for step, other in enumerate(others):
            copy = pltpu.make_async_remote_copy(
                src_ref=pick_src(other), dst_ref=pick_dst(me),
                send_sem=send_sem.at[a, step], recv_sem=recv_sem.at[a, step],
                device_id=member(other), device_id_type=MESH,
            )
            copy.start()
            line.append(copy)
        return local, line

    def swap_in(a, src, width, dst):
        return swap(a, lambda n: src.at[:, columns(width, n)], lambda n: dst.at[mine])

    def swap_out(a, src, width, dst):
        return swap(
            a,
            lambda n: src.at[pl.ds(pl.multiple_of(n * rows, rows), rows)],
            lambda n: dst.at[:, columns(width, n)],
        )

    def settle(pair):
        pair[0].wait()
        for copy in pair[1]:
            copy.wait_recv()

    def hop_in(step, c):
        return pltpu.make_async_remote_copy(
            src_ref=band.at[distance - step, c], dst_ref=band.at[distance - step - 1, c],
            send_sem=in_send.at[step, c], recv_sem=in_recv.at[step, c],
            device_id=(ctx + ctx_low, head), device_id_type=MESH,
        )

    def hop_out(step, c):
        return pltpu.make_async_remote_copy(
            src_ref=sums.at[step, c], dst_ref=landed.at[step, c],
            send_sem=out_send.at[step, c], recv_sem=out_recv.at[step, c],
            device_id=(ctx - ctx_low, head), device_id_type=MESH,
        )

    kv_swap = [
        swap_in(0, k_in, HD, band.at[distance, 0]),
        swap_in(1, v_in, HD, band.at[distance, 1]),
    ]
    qg_swap = [swap_in(2, q_in, q_cols, qo), swap_in(3, g_in, q_cols, go)]
    acc[...] = jnp.zeros_like(acc)
    dqt[...] = jnp.zeros_like(dqt)
    peak[...] = jnp.full_like(peak, -1e30)
    for c in range(2):
        settle(kv_swap[c])

        @pl.when(has_next)
        def _():
            hop_in(0, c).start()

    for pair in qg_swap:
        settle(pair)

    spans = [slice(h * TILE, (h + 1) * TILE) for h in range(share)]
    cols = [slice(h * HD, (h + 1) * HD) for h in range(share)]

    def tile_rows(i):
        return pl.ds(pl.multiple_of(i * TILE, TILE), TILE)

    def turn_rows(i, _):
        here = tile_rows(i)
        for h in range(share):
            qt[i, :, spans[h]] = qo[here, cols[h]].T
            gt[i, :, spans[h]] = go[here, cols[h]].T
        return 0

    lax.fori_loop(0, per_block, turn_rows, 0)

    def across(x, y):
        return lax.dot_general(
            x, y, (((1,), (1,)), ((), ())), preferred_element_type=jnp.float32
        )

    def fold(x, op):
        return op(x.reshape(TILE // 8, 8, TILE), 0)

    def score_slot(n, _):
        slot = distance - n

        @pl.when(block - n >= 0)
        def _():
            for c in range(2):
                @pl.when(n > 0)
                def _():
                    hop_in(n - 1, c).wait_recv()

                @pl.when((n > 0) & (n < distance) & has_next)
                def _():
                    hop_in(n, c).start()

            def key_step(t, _):
                kb = slot * per_block + t
                here = tile_rows(t)
                keys = band[slot, 0, here, :]
                kt[kb] = keys.T
                vt[kb] = band[slot, 1, here, :].T
                tile_token = first_token + kb * TILE
                col = tile_token + lax.broadcasted_iota(jnp.int32, (TILE, TILE), 0)

                def row_step(i, _):
                    starts = start_ref[i]
                    token = base + i * TILE + lax.broadcasted_iota(jnp.int32, (TILE, TILE), 1)
                    seen = (col >= starts) & (col <= token)
                    for h in range(share):
                        s = jnp.dot(keys, qt[i, :, spans[h]], preferred_element_type=jnp.float32)
                        s = jnp.where(seen, s, -1e30)
                        kept[i, kb - i, :, spans[h]] = s
                        peak[i, :, spans[h]] = jnp.maximum(peak[i, :, spans[h]], fold(s, jnp.max))
                    return 0

                lax.fori_loop(
                    jnp.maximum(kb - reach + 1, 0), jnp.minimum(kb + 1, per_block), row_step, 0
                )
                return 0

            lax.fori_loop(0, per_block, key_step, 0)

        return 0

    lax.fori_loop(0, distance + 1, score_slot, 0)

    def forward_tile(i, _):
        here = tile_rows(i)
        top = jnp.max(peak[i], 0, keepdims=True) * factor
        total[...] = jnp.zeros_like(total)
        ot[...] = jnp.zeros_like(ot)

        def forward(kb, _):
            values_t = vt[kb]
            for h in range(share):
                span = spans[h]
                p = jnp.exp2(kept[i, kb - i, :, span] * factor - top[:, span])
                kept[i, kb - i, :, span] = p
                total[:, span] += fold(p, jnp.sum)
                ot[:, span] += jnp.dot(
                    values_t, p.astype(jnp.bfloat16), preferred_element_type=jnp.float32
                )
            return 0

        lax.fori_loop(jnp.maximum(i, first_kb), i + reach, forward, 0)
        inverse = 1.0 / jnp.sum(total[...], 0, keepdims=True)
        out = ot[...] * inverse
        inv[i] = inverse
        delta[i] = jnp.sum(out * gt[i].astype(jnp.float32), 0, keepdims=True)
        for h in range(share):
            att[here, cols[h]] = out[:, spans[h]].T.astype(jnp.bfloat16)
        return 0

    lax.fori_loop(0, per_block, forward_tile, 0)
    att_swap = swap_out(4, att, q_cols, ao_ref)

    def back_slot(slot, _):
        @pl.when(block - (distance - slot) >= 0)
        def _():
            def key_step(t, _):
                kb = slot * per_block + t
                values = band[slot, 1, tile_rows(t), :]
                keys_t = kt[kb]

                def row_step(i, _):
                    inverse, shift = inv[i], delta[i]
                    for h in range(share):
                        span = spans[h]
                        w = kept[i, kb - i, :, span] * inverse[:, span]
                        dp = jnp.dot(values, gt[i, :, span], preferred_element_type=jnp.float32)
                        wide[0, :, span] = w.astype(jnp.bfloat16)
                        wide[1, :, span] = (w * (dp - shift[:, span])).astype(jnp.bfloat16)
                    dqt[i] += jnp.dot(keys_t, wide[1], preferred_element_type=jnp.float32)
                    dv = across(gt[i], wide[0])
                    dk = across(qt[i], wide[1])
                    acc[0, kb] += dk
                    acc[1, kb] += dv
                    return 0

                lax.fori_loop(
                    jnp.maximum(kb - reach + 1, 0), jnp.minimum(kb + 1, per_block), row_step, 0
                )
                return 0

            lax.fori_loop(0, per_block, key_step, 0)
            for c in range(2):
                by = scale if c == 0 else 1.0

                def term(t):
                    return (acc[c, slot * per_block + t] * by).T

                @pl.when((slot > 0) & has_next)
                def _():
                    hop_out(slot - 1, c).wait_recv()
                    for t in range(per_block):
                        rows_t = slice(t * TILE, (t + 1) * TILE)
                        both = term(t) + landed[slot - 1, c, rows_t, :].astype(jnp.float32)
                        sums[slot, c, rows_t, :] = both.astype(jnp.bfloat16)

                @pl.when(jnp.logical_not((slot > 0) & has_next))
                def _():
                    for t in range(per_block):
                        sums[slot, c, t * TILE:(t + 1) * TILE, :] = term(t).astype(jnp.bfloat16)

            for c in range(2):
                @pl.when(slot < distance)
                def _():
                    hop_out(slot, c).start()

        return 0

    lax.fori_loop(0, distance + 1, back_slot, 0)

    def turn_back(i, _):
        for h in range(share):
            dq[tile_rows(i), cols[h]] = (dqt[i, :, spans[h]] * scale).T.astype(jnp.bfloat16)
        return 0

    lax.fori_loop(0, per_block, turn_back, 0)
    out_swaps = [
        swap_out(5, dq, q_cols, do_ref),
        swap_out(6, sums.at[distance, 0], HD, ko_ref),
        swap_out(7, sums.at[distance, 1], HD, vo_ref),
    ]
    for pair in kv_swap + qg_swap:
        for copy in pair[1]:
            copy.wait_send()
    for pair in [att_swap] + out_swaps:
        settle(pair)
        for copy in pair[1]:
            copy.wait_send()
    for c in range(2):
        for step in range(distance):
            @pl.when((block - step >= 0) & has_next)
            def _():
                hop_in(step, c).wait_send()

            @pl.when(block - (distance - step) >= 0)
            def _():
                hop_out(step, c).wait_send()


def per_device(queries, keys, values, grad_out, doc_ids):
    heads = lax.axis_size("head")
    peers = lax.axis_size("ctx")
    rows = queries.shape[0]
    group = keys.shape[1] // HD
    share = queries.shape[1] // HD // group
    ctx_low = group // heads
    blocks = peers // ctx_low
    tokens = rows * group
    distance = DOC_MOST // tokens
    bf16, f32 = jnp.bfloat16, jnp.float32
    vmem = pl.BlockSpec(memory_space=pltpu.VMEM)
    hbm = pl.BlockSpec(memory_space=pl.ANY)
    dma = pltpu.SemaphoreType.DMA
    base = lax.axis_index("ctx") // ctx_low * tokens
    padded = jnp.concatenate((jnp.full((distance * tokens,), -1, jnp.int32), doc_ids), 0)
    window = lax.dynamic_slice_in_dim(padded, base, (distance + 1) * tokens, 0)
    mine = lax.dynamic_slice_in_dim(doc_ids, base, tokens, 0)
    starts = base - distance * tokens + jnp.sum(
        (window[:, None] < mine[None, :]).astype(jnp.int32), 0, dtype=jnp.int32
    )
    tiles = tokens // TILE
    span = share * TILE
    all_tiles = (distance + 1) * tiles
    return pl.pallas_call(
        functools.partial(fused_kernel, heads, ctx_low, blocks, distance, HD ** -0.5),
        out_shape=(
            jax.ShapeDtypeStruct(queries.shape, bf16),
            jax.ShapeDtypeStruct(queries.shape, bf16),
            jax.ShapeDtypeStruct(keys.shape, bf16),
            jax.ShapeDtypeStruct(keys.shape, bf16),
        ),
        in_specs=[vmem] + [hbm] * 4,
        out_specs=(hbm,) * 4,
        scratch_shapes=[
            pltpu.VMEM((tokens, share * HD), bf16),
            pltpu.VMEM((tokens, share * HD), bf16),
            pltpu.VMEM((distance + 1, 2, tokens, HD), bf16),
            pltpu.VMEM((2, all_tiles, HD, TILE), f32),
            pltpu.VMEM((tiles, distance * tiles + 1, TILE, span), f32),
            pltpu.VMEM((tiles, HD, span), bf16),
            pltpu.VMEM((tiles, HD, span), bf16),
            pltpu.VMEM((tiles, 8, span), f32),
            pltpu.VMEM((8, span), f32),
            pltpu.VMEM((HD, span), f32),
            pltpu.VMEM((tiles, HD, span), f32),
            pltpu.VMEM((all_tiles, HD, TILE), bf16),
            pltpu.VMEM((all_tiles, HD, TILE), bf16),
            pltpu.VMEM((tiles, 1, span), f32),
            pltpu.VMEM((tiles, 1, span), f32),
            pltpu.VMEM((tokens, share * HD), bf16),
            pltpu.VMEM((tokens, share * HD), bf16),
            pltpu.VMEM((distance + 1, 2, tokens, HD), bf16),
            pltpu.VMEM((distance, 2, tokens, HD), bf16),
            pltpu.VMEM((2, TILE, span), bf16),
            dma((8,)), dma((8, group - 1)), dma((8, group - 1)),
            dma((distance, 2)), dma((distance, 2)), dma((distance, 2)), dma((distance, 2)),
        ],
        compiler_params=pltpu.CompilerParams(
            collective_id=1, has_side_effects=True, vmem_limit_bytes=67043328
        ),
        name="fused",
    )(starts.reshape(tiles, 1, TILE), queries, keys, values, grad_out)


def solution(mesh):
    spec = P(("ctx", "head"), None)
    return jax.shard_map(
        per_device,
        mesh=mesh,
        in_specs=(spec, spec, spec, spec, P()),
        out_specs=(spec, spec, spec, spec),
        check_vma=False,
    )
```

profile of v0, /device:TPU:21, one launch (start us, length us, event | category | flops | bytes accessed | tf_op | source)
XLA Modules:
  0.0 130.0 jit_solution(6661785699345395245)
XLA Ops:
  0.7 0.7 dynamic_slice.7
  1.3 0.7 pad_dynamic-slice_fusion
  2.1 1.5 %convert_reduce_fusion = s32[1024]{0:T(1024)S(1)} fusion(s32[1024]{0:T(1024)S(1)} %dynamic_slice.7, s32[3072]{0:T(1024)S(1)} %pad_dynamic-slice_fusion), kind=kLoop, calls=%fused_computation | loop fusion | flops 9436160 | bytes 20480 | tf_op jit(solution)/shard_map/reduce_sum | solution.py:336
  3.5 0.6 broadcast_add_fusion
  4.1 121.0 %fused.1 = (bf16[128,4096]{1,0:T(8,128)(2,1)}, bf16[128,4096]{1,0:T(8,128)(2,1)}, bf16[128,1024]{1,0:T(8,128)(2,1)}, bf16[128,1024]{1,0:T(8,128)(2,1)}) custom-call(s32[4,1,256]{2,1,0:T(1,128)} %bitcast.1, bf16[128,4096]{1,0:T(8,128)(2,1)} %q_in.1, bf16[128,1024]{1,0:T(8,128)(2,1)} %k_in.1, bf16[128,1024]{1,0:T(8,128)(2,1)} %v_in.1, bf16[128,4096]{1,0:T(8,128)(2,1)} %g_in.1), custom_call_target="tpu_custom_call" | custom-call | tf_op jit(solution)/shard_map/fused/pallas_call | solution.py:342
  125.2 0.0 copy-start
  125.2 2.4 %copy.13 = bf16[128,4096]{1,0:T(8,128)(2,1)} copy(bf16[128,4096]{1,0:T(8,128)(2,1)} %get-tuple-element.8) | data formatting | bytes 2097152
  127.5 0.0 copy-done
  127.5 0.0 copy-start.2
  127.5 0.0 copy-start.1
  127.5 1.0 copy.14
  128.5 0.1 copy-done.2
  128.6 0.7 copy.15
  129.3 0.0 copy-done.1
  129.3 0.7 copy.16
Async XLA Ops:
  125.2 2.4 %copy-start = (bf16[128,4096]{1,0:T(8,128)(2,1)S(1)}, bf16[128,4096]{1,0:T(8,128)(2,1)}, u32[]{:S(2)}) copy-start(bf16[128,4096]{1,0:T(8,128)(2,1)} %get-tuple-element.9) | copy-start | bytes 3145732
  127.5 1.1 copy-start.2
  127.5 1.8 %copy-start.1 = (bf16[128,1024]{1,0:T(8,128)(2,1)S(1)}, bf16[128,1024]{1,0:T(8,128)(2,1)}, u32[]{:S(2)}) copy-start(bf16[128,1024]{1,0:T(8,128)(2,1)} %get-tuple-element.11) | copy-start | bytes 786436
where the time goes:
time: 132 us; the launch traced here: 130 us
  Pallas kernels  121 us (92%)
  local copies, waits for them, and re-layouts  6.28 us (5%)
  other arithmetic  2.05 us (2%)
    pallas_call x1, Pallas kernels, per_device(): pl.pallas_call(functools.partial(fused_kernel, heads, ctx_low, blocks, di...  121 us
    unnamed x10, local copies, waits for them, and re-layouts  4.88 us

commit v1 on v0

v1 whole, which is shorter than its diff:
```python
import functools

import jax
import jax.numpy as jnp
from jax import lax
from jax.experimental import pallas as pl
from jax.experimental.pallas import tpu as pltpu
from jax.sharding import PartitionSpec as P

HD = 128
DOC_MOST = 2048
TILE = 256
LOG2E = 1.4426950408889634
MESH = pl.DeviceIdType.MESH


def place(ctx_low, heads):
    ctx, head = lax.axis_index("ctx"), lax.axis_index("head")
    block = ctx // ctx_low
    me = (ctx - block * ctx_low) * heads + head

    def member(number):
        return (block * ctx_low + number // heads, lax.rem(number, heads))

    return ctx, head, block, me, member


def greet(members, ctx, head, ctx_low, has_prev, has_next):
    barrier = pltpu.get_barrier_semaphore()
    for device in members:
        pl.semaphore_signal(barrier, inc=1, device_id=device, device_id_type=MESH)

    @pl.when(has_prev)
    def _():
        pl.semaphore_signal(barrier, inc=1, device_id=(ctx - ctx_low, head), device_id_type=MESH)

    @pl.when(has_next)
    def _():
        pl.semaphore_signal(barrier, inc=1, device_id=(ctx + ctx_low, head), device_id_type=MESH)

    near = has_prev.astype(jnp.int32) + has_next.astype(jnp.int32)
    pl.semaphore_wait(barrier, len(members) + near)


def fused_kernel(
    heads, ctx_low, blocks, distance, scale,
    doc_ref, q_in, k_in, v_in, g_in,
    ao_ref, do_ref, ko_ref, vo_ref,
    qo, go, band, acc, kept, peak, total, ot, dqt, kt, vt, inv, delta,
    att, dq, sums, landed, wide, seen_doc,
    own_sem, send_sem, recv_sem, in_send, in_recv, out_send, out_recv,
):
    group = ctx_low * heads
    rows = q_in.shape[0]
    q_cols = q_in.shape[1] // group
    tokens = qo.shape[0] * TILE
    share = q_cols // HD
    factor = scale * LOG2E
    per_block = tokens // TILE
    per_tile = TILE // rows
    reach = distance * per_block + 1
    ctx, head, block, me, member = place(ctx_low, heads)
    has_prev, has_next = block > 0, block < blocks - 1
    others = [lax.rem(me + step, group) for step in range(1, group)]
    greet([member(o) for o in others], ctx, head, ctx_low, has_prev, has_next)
    my_tile = me // per_tile
    my_row = (me - my_tile * per_tile) * rows
    mine = pl.ds(pl.multiple_of(me * rows, rows), rows)
    first_tile = (block - distance) * per_block
    first_kb = jnp.maximum(distance - block, 0) * per_block

    def columns(width, number):
        return pl.ds(pl.multiple_of(number * width, width), width)

    def swap_in(a, src, first, width, dst):
        def part(number):
            return src.at[:, pl.ds(pl.multiple_of(number * width + first, HD), HD)]

        local = pltpu.make_async_copy(part(me), dst, own_sem.at[a])
        local.start()
        line = []
        for step, other in enumerate(others):
            copy = pltpu.make_async_remote_copy(
                src_ref=part(other), dst_ref=dst,
                send_sem=send_sem.at[a, step], recv_sem=recv_sem.at[a, step],
                device_id=member(other), device_id_type=MESH,
            )
            copy.start()
            line.append(copy)
        return local, line

    def head_rows(h):
        return pl.ds(pl.multiple_of(h * TILE + my_row, rows), rows)

    def settle(pair):
        pair[0].wait()
        for copy in pair[1]:
            copy.wait_recv()

    def tile_out(a, i, src, width, dst):
        def one(j, _):
            number = i * per_tile + j
            step = lax.rem(number - me + group, group)
            piece = src.at[pl.ds(pl.multiple_of(number * rows, rows), rows)]
            place_there = dst.at[:, columns(width, me)]

            @pl.when(step == 0)
            def _():
                pltpu.make_async_copy(piece, place_there, own_sem.at[a]).start()

            @pl.when(step > 0)
            def _():
                pltpu.make_async_remote_copy(
                    src_ref=piece, dst_ref=place_there,
                    send_sem=send_sem.at[a, step - 1], recv_sem=recv_sem.at[a, step - 1],
                    device_id=member(number), device_id_type=MESH,
                ).start()

            return 0

        lax.fori_loop(0, per_tile, one, 0)

    def end_out(a, src, width, dst):
        piece, place_there = src.at[mine], dst.at[:, columns(width, me)]
        pltpu.make_async_copy(piece, place_there, own_sem.at[a]).wait()
        for step, other in enumerate(others):
            copy = pltpu.make_async_remote_copy(
                src_ref=src.at[pl.ds(pl.multiple_of(other * rows, rows), rows)],
                dst_ref=place_there,
                send_sem=send_sem.at[a, step], recv_sem=recv_sem.at[a, step],
                device_id=member(other), device_id_type=MESH,
            )
            copy.wait_recv()
            copy.wait_send()

    def hop_in(step, c):
        return pltpu.make_async_remote_copy(
            src_ref=band.at[distance - step, c], dst_ref=band.at[distance - step - 1, c],
            send_sem=in_send.at[step, c], recv_sem=in_recv.at[step, c],
            device_id=(ctx + ctx_low, head), device_id_type=MESH,
        )

    def hop_out(step, c, t):
        return pltpu.make_async_remote_copy(
            src_ref=sums.at[step, c, tile_rows(t)], dst_ref=landed.at[step, c, tile_rows(t)],
            send_sem=out_send.at[step, c, t], recv_sem=out_recv.at[step, c, t],
            device_id=(ctx - ctx_low, head), device_id_type=MESH,
        )

    def tile_rows(i):
        return pl.ds(pl.multiple_of(i * TILE, TILE), TILE)

    kv_swap = [
        swap_in(0, k_in, 0, HD, band.at[distance, 0, mine]),
        swap_in(1, v_in, 0, HD, band.at[distance, 1, mine]),
    ]
    q_swap = [
        swap_in(2 + h, q_in, h * HD, q_cols, qo.at[my_tile, head_rows(h)]) for h in range(share)
    ]
    g_swap = [
        swap_in(2 + share + h, g_in, h * HD, q_cols, go.at[my_tile, head_rows(h)])
        for h in range(share)
    ]
    out_at = 2 + 2 * share
    acc[...] = jnp.zeros_like(acc)
    dqt[...] = jnp.zeros_like(dqt)
    peak[...] = jnp.full_like(peak, -1e30)
    for c in range(2):
        settle(kv_swap[c])

        @pl.when(has_next)
        def _():
            hop_in(0, c).start()

    for step in range(1, distance):
        @pl.when(block - step >= 0)
        def _():
            for c in range(2):
                hop_in(step - 1, c).wait_recv()

                @pl.when(has_next)
                def _():
                    hop_in(step, c).start()

    for pair in q_swap:
        settle(pair)

    spans = [slice(h * TILE, (h + 1) * TILE) for h in range(share)]
    cols = [slice(h * HD, (h + 1) * HD) for h in range(share)]

    def across(x, y):
        return lax.dot_general(
            x, y, (((1,), (1,)), ((), ())), preferred_element_type=jnp.float32
        )

    def fold(x, op):
        return op(x.reshape(TILE // 8, 8, TILE), 0)

    def score_slot(n, _):
        slot = distance - n

        @pl.when(block - n >= 0)
        def _():
            @pl.when(n == distance)
            def _():
                for c in range(2):
                    hop_in(distance - 1, c).wait_recv()

            def key_step(t, _):
                kb = slot * per_block + t
                here = tile_rows(t)
                keys = band[slot, 0, here, :]
                kt[kb] = keys.T
                vt[kb] = band[slot, 1, here, :].T
                docs = jnp.broadcast_to(doc_ref[first_tile + kb], (HD, TILE))
                seen_doc[...] = docs.T

                def row_step(i, _):
                    away = lax.broadcasted_iota(jnp.int32, (TILE, TILE), 1) - (
                        lax.broadcasted_iota(jnp.int32, (TILE, TILE), 0)
                    )
                    theirs = seen_doc[...]
                    same = jnp.concatenate([theirs, theirs], 1) == doc_ref[block * per_block + i]
                    seen = same & (away >= (kb - i - reach + 1) * TILE)
                    for h in range(share):
                        s = across(keys, qo[i, spans[h], :])
                        s = jnp.where(seen, s, -1e30)
                        kept[i, kb - i, :, spans[h]] = s
                        peak[i, :, spans[h]] = jnp.maximum(peak[i, :, spans[h]], fold(s, jnp.max))
                    return 0

                lax.fori_loop(
                    jnp.maximum(kb - reach + 1, 0), jnp.minimum(kb + 1, per_block), row_step, 0
                )
                return 0

            lax.fori_loop(0, per_block, key_step, 0)

        return 0

    lax.fori_loop(0, distance + 1, score_slot, 0)
    for pair in g_swap:
        settle(pair)

    def forward_tile(i, _):
        here = tile_rows(i)
        top = jnp.max(peak[i], 0, keepdims=True) * factor
        total[...] = jnp.zeros_like(total)
        ot[...] = jnp.zeros_like(ot)

        def forward(kb, _):
            values_t = vt[kb]
            for h in range(share):
                span = spans[h]
                p = jnp.exp2(kept[i, kb - i, :, span] * factor - top[:, span])
                kept[i, kb - i, :, span] = p
                total[:, span] += fold(p, jnp.sum)
                ot[:, span] += jnp.dot(
                    values_t, p.astype(jnp.bfloat16), preferred_element_type=jnp.float32
                )
            return 0

        lax.fori_loop(jnp.maximum(i, first_kb), i + reach, forward, 0)
        inverse = 1.0 / jnp.sum(total[...], 0, keepdims=True)
        inv[i] = inverse
        for h in range(share):
            out = ot[:, spans[h]] * inverse[:, spans[h]]
            grads = go[i, spans[h], :].T.astype(jnp.float32)
            delta[i, :, spans[h]] = jnp.sum(out * grads, 0, keepdims=True)
            att[here, cols[h]] = out.T.astype(jnp.bfloat16)
        tile_out(out_at, i, att, q_cols, ao_ref)
        return 0

    lax.fori_loop(0, per_block, forward_tile, 0)

    def back_slot(slot, _):
        @pl.when(block - (distance - slot) >= 0)
        def _():
            def key_step(t, _):
                kb = slot * per_block + t
                values = band[slot, 1, tile_rows(t), :]
                keys_t = kt[kb]

                def row_step(i, _):
                    inverse, shift = inv[i], delta[i]
                    for h in range(share):
                        span = spans[h]
                        w = kept[i, kb - i, :, span] * inverse[:, span]
                        dp = across(values, go[i, span, :])
                        wide[0, :, span] = w.astype(jnp.bfloat16)
                        wide[1, :, span] = (w * (dp - shift[:, span])).astype(jnp.bfloat16)
                    dqt[i] += jnp.dot(keys_t, wide[1], preferred_element_type=jnp.float32)
                    acc[0, kb] += jnp.dot(wide[1], qo[i], preferred_element_type=jnp.float32)
                    acc[1, kb] += jnp.dot(wide[0], go[i], preferred_element_type=jnp.float32)
                    return 0

                lax.fori_loop(
                    jnp.maximum(kb - reach + 1, 0), jnp.minimum(kb + 1, per_block), row_step, 0
                )

                @pl.when(slot < distance)
                def _():
                    send_term(slot, t)

                @pl.when(slot == distance)
                def _():
                    for h in range(share):
                        dq[tile_rows(t), cols[h]] = (
                            (dqt[t, :, spans[h]] * scale).T.astype(jnp.bfloat16)
                        )
                    tile_out(out_at + 1, t, dq, q_cols, do_ref)

                return 0

            lax.fori_loop(0, per_block, key_step, 0)

        return 0

    def close_term(slot, c, t):
        by = scale if c == 0 else 1.0
        term = acc[c, slot * per_block + t] * by

        @pl.when((slot > 0) & has_next)
        def _():
            hop_out(slot - 1, c, t).wait_recv()
            both = term + landed[slot - 1, c, tile_rows(t), :].astype(jnp.float32)
            sums[slot, c, tile_rows(t), :] = both.astype(jnp.bfloat16)

        @pl.when(jnp.logical_not((slot > 0) & has_next))
        def _():
            sums[slot, c, tile_rows(t), :] = term.astype(jnp.bfloat16)

    def send_term(slot, t):
        for c in range(2):
            close_term(slot, c, t)
        for c in range(2):
            hop_out(slot, c, t).start()

    lax.fori_loop(0, distance + 1, back_slot, 0)

    def finish(t, _):
        for c in range(2):
            close_term(distance, c, t)
        tile_out(out_at + 2, t, sums.at[distance, 0], HD, ko_ref)
        tile_out(out_at + 3, t, sums.at[distance, 1], HD, vo_ref)
        return 0

    lax.fori_loop(0, per_block, finish, 0)
    for pair in kv_swap + q_swap + g_swap:
        for copy in pair[1]:
            copy.wait_send()
    end_out(out_at, att, q_cols, ao_ref)
    end_out(out_at + 1, dq, q_cols, do_ref)
    end_out(out_at + 2, sums.at[distance, 0], HD, ko_ref)
    end_out(out_at + 3, sums.at[distance, 1], HD, vo_ref)
    for c in range(2):
        for step in range(distance):
            @pl.when((block - step >= 0) & has_next)
            def _():
                hop_in(step, c).wait_send()

            @pl.when(block - (distance - step) >= 0)
            def _():
                for t in range(per_block):
                    hop_out(step, c, t).wait_send()


def per_device(queries, keys, values, grad_out, doc_ids):
    heads = lax.axis_size("head")
    peers = lax.axis_size("ctx")
    rows = queries.shape[0]
    group = keys.shape[1] // HD
    share = queries.shape[1] // HD // group
    ctx_low = group // heads
    blocks = peers // ctx_low
    tokens = rows * group
    distance = DOC_MOST // tokens
    bf16, f32 = jnp.bfloat16, jnp.float32
    vmem = pl.BlockSpec(memory_space=pltpu.VMEM)
    hbm = pl.BlockSpec(memory_space=pl.ANY)
    dma = pltpu.SemaphoreType.DMA
    tiles = tokens // TILE
    span = share * TILE
    all_tiles = (distance + 1) * tiles
    swaps = 2 + 2 * share + 4
    return pl.pallas_call(
        functools.partial(fused_kernel, heads, ctx_low, blocks, distance, HD ** -0.5),
        out_shape=(
            jax.ShapeDtypeStruct(queries.shape, bf16),
            jax.ShapeDtypeStruct(queries.shape, bf16),
            jax.ShapeDtypeStruct(keys.shape, bf16),
            jax.ShapeDtypeStruct(keys.shape, bf16),
        ),
        in_specs=[vmem] + [hbm] * 4,
        out_specs=(hbm,) * 4,
        scratch_shapes=[
            pltpu.VMEM((tiles, span, HD), bf16),
            pltpu.VMEM((tiles, span, HD), bf16),
            pltpu.VMEM((distance + 1, 2, tokens, HD), bf16),
            pltpu.VMEM((2, all_tiles, TILE, HD), f32),
            pltpu.VMEM((tiles, distance * tiles + 1, TILE, span), f32),
            pltpu.VMEM((tiles, 8, span), f32),
            pltpu.VMEM((8, span), f32),
            pltpu.VMEM((HD, span), f32),
            pltpu.VMEM((tiles, HD, span), f32),
            pltpu.VMEM((all_tiles, HD, TILE), bf16),
            pltpu.VMEM((all_tiles, HD, TILE), bf16),
            pltpu.VMEM((tiles, 1, span), f32),
            pltpu.VMEM((tiles, 1, span), f32),
            pltpu.VMEM((tokens, share * HD), bf16),
            pltpu.VMEM((tokens, share * HD), bf16),
            pltpu.VMEM((distance + 1, 2, tokens, HD), bf16),
            pltpu.VMEM((distance, 2, tokens, HD), bf16),
            pltpu.VMEM((2, TILE, span), bf16),
            pltpu.VMEM((TILE, HD), jnp.int32),
            dma((swaps,)), dma((swaps, group - 1)), dma((swaps, group - 1)),
            dma((distance, 2)), dma((distance, 2)),
            dma((distance, 2, tiles)), dma((distance, 2, tiles)),
        ],
        compiler_params=pltpu.CompilerParams(
            collective_id=1, has_side_effects=True, vmem_limit_bytes=67043328
        ),
        name="fused",
    )(doc_ids.reshape(-1, 1, TILE), queries, keys, values, grad_out)


def solution(mesh):
    spec = P(("ctx", "head"), None)
    return jax.shard_map(
        per_device,
        mesh=mesh,
        in_specs=(spec, spec, spec, spec, P()),
        out_specs=(spec, spec, spec, spec),
        check_vma=False,
    )
```

time: 132 us -> 105 us (0.80); the launches traced: 130 us -> 105 us
  Pallas kernels: 121 us -> 98.9 us
  other arithmetic: 2.05 us -> 0 us
    pallas_call x1, Pallas kernels: 121 us -> 98.9 us  [per_device(): pl.pallas_call(functools.partial(fused_kernel, heads, ctx_low, blocks, di...]
    reduce_sum x1 -> x0, other arithmetic: 1.45 us -> none  [per_device(): jnp.sum((window[:, None] < mine[None, :]).astype(jnp.int32), 0, dtype=jnp...]
    dynamic_slice x2 -> x0, local copies, waits for them, and re-layouts: 1.4 us -> none  [the longest x1 0.71 us: per_device(): window = lax.dynamic_slice_in_dim(padded, base, (distance + 1) * tokens, 0)]
where the time goes in v1:
time: 105 us
  Pallas kernels  98.9 us (94%)
  local copies, waits for them, and re-layouts  5.22 us (5%)
    pallas_call x1, Pallas kernels, per_device(): pl.pallas_call(functools.partial(fused_kernel, heads, ctx_low, blocks, di...  98.9 us
    unnamed x10, local copies, waits for them, and re-layouts  5.22 us

profile of v1, /device:TPU:21, one launch (start us, length us, event | category | flops | bytes accessed | tf_op | source)
XLA Modules:
  0.0 104.7 jit_solution(6154321548915587806)
XLA Ops:
  0.6 98.9 %fused.1 = (bf16[128,4096]{1,0:T(8,128)(2,1)}, bf16[128,4096]{1,0:T(8,128)(2,1)}, bf16[128,1024]{1,0:T(8,128)(2,1)}, bf16[128,1024]{1,0:T(8,128)(2,1)}) custom-call(s32[16,1,256]{2,1,0:T(1,128)} %bitcast.1, bf16[128,4096]{1,0:T(8,128)(2,1)} %q_in.1, bf16[128,1024]{1,0:T(8,128)(2,1)} %k_in.1, bf16[128,1024]{1,0:T(8,128)(2,1)} %v_in.1, bf16[128,4096]{1,0:T(8,128)(2,1)} %g_in.1), custom_call_target="tpu_custom_call" | custom-call | tf_op jit(solution)/shard_map/fused/pallas_call | solution.py:386
  99.5 0.0 copy-start
  99.5 2.4 %copy.13 = bf16[128,4096]{1,0:T(8,128)(2,1)} copy(bf16[128,4096]{1,0:T(8,128)(2,1)} %get-tuple-element.8) | data formatting | bytes 2097152
  101.9 0.0 copy-done
  101.9 0.0 copy-start.2
  101.9 1.0 copy.14
  102.9 0.1 copy-done.2
  103.0 0.0 copy-start.1
  103.0 0.7 copy.15
  103.7 0.3 copy-done.1
  104.0 0.7 copy.16
Async XLA Ops:
  99.5 2.4 %copy-start = (bf16[128,4096]{1,0:T(8,128)(2,1)S(1)}, bf16[128,4096]{1,0:T(8,128)(2,1)}, u32[]{:S(2)}) copy-start(bf16[128,4096]{1,0:T(8,128)(2,1)} %get-tuple-element.9) | copy-start | bytes 3145732
  101.9 1.1 %copy-start.2 = (bf16[128,1024]{1,0:T(8,128)(2,1)S(1)}, bf16[128,1024]{1,0:T(8,128)(2,1)}, u32[]{:S(2)}) copy-start(bf16[128,1024]{1,0:T(8,128)(2,1)} %get-tuple-element.10) | copy-start | bytes 786436
  103.0 1.0 copy-start.1

commit v2 on v1

--- a/solution.py
+++ b/solution.py
@@ -46,8 +46,8 @@
     heads, ctx_low, blocks, distance, scale,
     doc_ref, q_in, k_in, v_in, g_in,
     ao_ref, do_ref, ko_ref, vo_ref,
-    qo, go, band, acc, kept, peak, total, ot, dqt, kt, vt, inv, delta,
-    att, dq, sums, landed, wide, seen_doc,
+    qo, go, band, acc, kept, peak, total, made, dqs, qt, gt, inv, delta,
+    att, dq, sums, landed, wide, row_doc,
     own_sem, send_sem, recv_sem, in_send, in_recv, out_send, out_recv,
 ):
     group = ctx_low * heads
@@ -163,8 +163,10 @@
     ]
     out_at = 2 + 2 * share
     acc[...] = jnp.zeros_like(acc)
-    dqt[...] = jnp.zeros_like(dqt)
+    dqs[...] = jnp.zeros_like(dqs)
     peak[...] = jnp.full_like(peak, -1e30)
+    for i in range(per_block):
+        row_doc[i] = jnp.broadcast_to(doc_ref[block * per_block + i], (HD, TILE)).T
     for c in range(2):
         settle(kv_swap[c])
 
@@ -193,8 +195,8 @@
             x, y, (((1,), (1,)), ((), ())), preferred_element_type=jnp.float32
         )
 
-    def fold(x, op):
-        return op(x.reshape(TILE // 8, 8, TILE), 0)
+    def twice(x):
+        return jnp.concatenate([x, x], 1)
 
     def score_slot(n, _):
         slot = distance - n
@@ -208,25 +210,19 @@
 
             def key_step(t, _):
                 kb = slot * per_block + t
-                here = tile_rows(t)
-                keys = band[slot, 0, here, :]
-                kt[kb] = keys.T
-                vt[kb] = band[slot, 1, here, :].T
-                docs = jnp.broadcast_to(doc_ref[first_tile + kb], (HD, TILE))
-                seen_doc[...] = docs.T
 
                 def row_step(i, _):
-                    away = lax.broadcasted_iota(jnp.int32, (TILE, TILE), 1) - (
-                        lax.broadcasted_iota(jnp.int32, (TILE, TILE), 0)
+                    keys = band[slot, 0, tile_rows(t), :]
+                    away = lax.broadcasted_iota(jnp.int32, (TILE, TILE), 0) - (
+                        lax.broadcasted_iota(jnp.int32, (TILE, TILE), 1)
                     )
-                    theirs = seen_doc[...]
-                    same = jnp.concatenate([theirs, theirs], 1) == doc_ref[block * per_block + i]
+                    same = twice(row_doc[i]) == doc_ref[first_tile + kb]
                     seen = same & (away >= (kb - i - reach + 1) * TILE)
                     for h in range(share):
-                        s = across(keys, qo[i, spans[h], :])
-                        s = jnp.where(seen, s, -1e30)
-                        kept[i, kb - i, :, spans[h]] = s
-                        peak[i, :, spans[h]] = jnp.maximum(peak[i, :, spans[h]], fold(s, jnp.max))
+                        s = jnp.where(seen, across(qo[i, spans[h], :], keys), -1e30)
+                        kept[i, kb - i, spans[h], :] = s
+                        both = jnp.maximum(s[:, :HD], s[:, HD:])
+                        peak[i, spans[h], :] = jnp.maximum(peak[i, spans[h], :], both)
                     return 0
 
                 lax.fori_loop(
@@ -244,30 +240,36 @@
 
     def forward_tile(i, _):
         here = tile_rows(i)
-        top = jnp.max(peak[i], 0, keepdims=True) * factor
+        for h in range(share):
+            top = jnp.max(peak[i, spans[h], :], 1, keepdims=True) * factor
+            peak[i, spans[h], :] = jnp.broadcast_to(top, (TILE, HD))
         total[...] = jnp.zeros_like(total)
-        ot[...] = jnp.zeros_like(ot)
+        made[...] = jnp.zeros_like(made)
 
         def forward(kb, _):
-            values_t = vt[kb]
+            slot = kb // per_block
+            values = band[slot, 1, tile_rows(kb - slot * per_block), :]
             for h in range(share):
                 span = spans[h]
-                p = jnp.exp2(kept[i, kb - i, :, span] * factor - top[:, span])
-                kept[i, kb - i, :, span] = p
-                total[:, span] += fold(p, jnp.sum)
-                ot[:, span] += jnp.dot(
-                    values_t, p.astype(jnp.bfloat16), preferred_element_type=jnp.float32
+                p = jnp.exp2(kept[i, kb - i, span, :] * factor - twice(peak[i, span, :]))
+                kept[i, kb - i, span, :] = p
+                total[span, :] += p[:, :HD] + p[:, HD:]
+                made[span, :] += jnp.dot(
+                    p.astype(jnp.bfloat16), values, preferred_element_type=jnp.float32
                 )
             return 0
 
         lax.fori_loop(jnp.maximum(i, first_kb), i + reach, forward, 0)
-        inverse = 1.0 / jnp.sum(total[...], 0, keepdims=True)
-        inv[i] = inverse
         for h in range(share):
-            out = ot[:, spans[h]] * inverse[:, spans[h]]
-            grads = go[i, spans[h], :].T.astype(jnp.float32)
-            delta[i, :, spans[h]] = jnp.sum(out * grads, 0, keepdims=True)
-            att[here, cols[h]] = out.T.astype(jnp.bfloat16)
+            span = spans[h]
+            inverse = 1.0 / jnp.sum(total[span, :], 1, keepdims=True)
+            inv[i, span, :] = jnp.broadcast_to(inverse, (TILE, HD))
+            out = made[span, :] * inverse
+            shift = jnp.sum(out * go[i, span, :].astype(jnp.float32), 1, keepdims=True)
+            delta[i, span, :] = jnp.broadcast_to(shift, (TILE, HD))
+            att[here, cols[h]] = out.astype(jnp.bfloat16)
+            qt[i, :, span] = qo[i, span, :].T
+            gt[i, :, span] = go[i, span, :].T
         tile_out(out_at, i, att, q_cols, ao_ref)
         return 0
 
@@ -278,20 +280,22 @@
         def _():
             def key_step(t, _):
                 kb = slot * per_block + t
-                values = band[slot, 1, tile_rows(t), :]
-                keys_t = kt[kb]
 
                 def row_step(i, _):
-                    inverse, shift = inv[i], delta[i]
+                    keys = band[slot, 0, tile_rows(t), :]
+                    values = band[slot, 1, tile_rows(t), :]
                     for h in range(share):
                         span = spans[h]
-                        w = kept[i, kb - i, :, span] * inverse[:, span]
-                        dp = across(values, go[i, span, :])
-                        wide[0, :, span] = w.astype(jnp.bfloat16)
-                        wide[1, :, span] = (w * (dp - shift[:, span])).astype(jnp.bfloat16)
-                    dqt[i] += jnp.dot(keys_t, wide[1], preferred_element_type=jnp.float32)
-                    acc[0, kb] += jnp.dot(wide[1], qo[i], preferred_element_type=jnp.float32)
-                    acc[1, kb] += jnp.dot(wide[0], go[i], preferred_element_type=jnp.float32)
+                        w = kept[i, kb - i, span, :] * twice(inv[i, span, :])
+                        dp = across(go[i, span, :], values)
+                        wide[0, span, :] = w.astype(jnp.bfloat16)
+                        wide[1, span, :] = (w * (dp - twice(delta[i, span, :]))).astype(jnp.bfloat16)
+                    for h in range(share):
+                        dqs[i, spans[h], :] += jnp.dot(
+                            wide[1, spans[h], :], keys, preferred_element_type=jnp.float32
+                        )
+                    acc[0, kb] += jnp.dot(qt[i], wide[1], preferred_element_type=jnp.float32)
+                    acc[1, kb] += jnp.dot(gt[i], wide[0], preferred_element_type=jnp.float32)
                     return 0
 
                 lax.fori_loop(
@@ -305,9 +309,7 @@
                 @pl.when(slot == distance)
                 def _():
                     for h in range(share):
-                        dq[tile_rows(t), cols[h]] = (
-                            (dqt[t, :, spans[h]] * scale).T.astype(jnp.bfloat16)
-                        )
+                        dq[tile_rows(t), cols[h]] = (dqs[t, spans[h], :] * scale).astype(jnp.bfloat16)
                     tile_out(out_at + 1, t, dq, q_cols, do_ref)
 
                 return 0
@@ -318,7 +320,7 @@
 
     def close_term(slot, c, t):
         by = scale if c == 0 else 1.0
-        term = acc[c, slot * per_block + t] * by
+        term = (acc[c, slot * per_block + t] * by).T
 
         @pl.when((slot > 0) & has_next)
         def _():
@@ -397,22 +399,22 @@
             pltpu.VMEM((tiles, span, HD), bf16),
             pltpu.VMEM((tiles, span, HD), bf16),
             pltpu.VMEM((distance + 1, 2, tokens, HD), bf16),
-            pltpu.VMEM((2, all_tiles, TILE, HD), f32),
-            pltpu.VMEM((tiles, distance * tiles + 1, TILE, span), f32),
-            pltpu.VMEM((tiles, 8, span), f32),
-            pltpu.VMEM((8, span), f32),
-            pltpu.VMEM((HD, span), f32),
-            pltpu.VMEM((tiles, HD, span), f32),
-            pltpu.VMEM((all_tiles, HD, TILE), bf16),
-            pltpu.VMEM((all_tiles, HD, TILE), bf16),
-            pltpu.VMEM((tiles, 1, span), f32),
-            pltpu.VMEM((tiles, 1, span), f32),
+            pltpu.VMEM((2, all_tiles, HD, TILE), f32),
+            pltpu.VMEM((tiles, distance * tiles + 1, span, TILE), f32),
+            pltpu.VMEM((tiles, span, HD), f32),
+            pltpu.VMEM((span, HD), f32),
+            pltpu.VMEM((span, HD), f32),
+            pltpu.VMEM((tiles, span, HD), f32),
+            pltpu.VMEM((tiles, HD, span), bf16),
+            pltpu.VMEM((tiles, HD, span), bf16),
+            pltpu.VMEM((tiles, span, HD), f32),
+            pltpu.VMEM((tiles, span, HD), f32),
             pltpu.VMEM((tokens, share * HD), bf16),
             pltpu.VMEM((tokens, share * HD), bf16),
             pltpu.VMEM((distance + 1, 2, tokens, HD), bf16),
             pltpu.VMEM((distance, 2, tokens, HD), bf16),
-            pltpu.VMEM((2, TILE, span), bf16),
-            pltpu.VMEM((TILE, HD), jnp.int32),
+            pltpu.VMEM((2, span, TILE), bf16),
+            pltpu.VMEM((tiles, TILE, HD), jnp.int32),
             dma((swaps,)), dma((swaps, group - 1)), dma((swaps, group - 1)),
             dma((distance, 2)), dma((distance, 2)),
             dma((distance, 2, tiles)), dma((distance, 2, tiles)),

time: 105 us -> 101 us (0.962)
  Pallas kernels: 98.9 us -> 94.7 us
    pallas_call x1, Pallas kernels: 98.9 us -> 94.7 us  [per_device(): pl.pallas_call(functools.partial(fused_kernel, heads, ctx_low, blocks, di...]
where the time goes in v2:
time: 101 us
  Pallas kernels  94.7 us (94%)
  local copies, waits for them, and re-layouts  5.22 us (5%)
    pallas_call x1, Pallas kernels, per_device(): pl.pallas_call(functools.partial(fused_kernel, heads, ctx_low, blocks, di...  94.7 us
    unnamed x10, local copies, waits for them, and re-layouts  5.22 us

profile of v2, /device:TPU:21, one launch (start us, length us, event | category | flops | bytes accessed | tf_op | source)
XLA Modules:
  0.0 100.6 jit_solution(1667975740160550828)
XLA Ops:
  0.6 94.7 %fused.1 = (bf16[128,4096]{1,0:T(8,128)(2,1)}, bf16[128,4096]{1,0:T(8,128)(2,1)}, bf16[128,1024]{1,0:T(8,128)(2,1)}, bf16[128,1024]{1,0:T(8,128)(2,1)}) custom-call(s32[16,1,256]{2,1,0:T(1,128)} %bitcast.1, bf16[128,4096]{1,0:T(8,128)(2,1)} %q_in.1, bf16[128,1024]{1,0:T(8,128)(2,1)} %k_in.1, bf16[128,1024]{1,0:T(8,128)(2,1)} %v_in.1, bf16[128,4096]{1,0:T(8,128)(2,1)} %g_in.1), custom_call_target="tpu_custom_call" | custom-call | tf_op jit(solution)/shard_map/fused/pallas_call | solution.py:388
  95.4 0.0 copy-start
  95.4 2.4 %copy.13 = bf16[128,4096]{1,0:T(8,128)(2,1)} copy(bf16[128,4096]{1,0:T(8,128)(2,1)} %get-tuple-element.8) | data formatting | bytes 2097152
  97.8 0.0 copy-done
  97.8 0.0 copy-start.2
  97.8 1.0 copy.14
  98.7 0.1 copy-done.2
  98.9 0.0 copy-start.1
  98.9 0.7 copy.15
  99.6 0.3 copy-done.1
  99.9 0.7 copy.16
Async XLA Ops:
  95.4 2.4 %copy-start = (bf16[128,4096]{1,0:T(8,128)(2,1)S(1)}, bf16[128,4096]{1,0:T(8,128)(2,1)}, u32[]{:S(2)}) copy-start(bf16[128,4096]{1,0:T(8,128)(2,1)} %get-tuple-element.9) | copy-start | bytes 3145732
  97.8 1.1 %copy-start.2 = (bf16[128,1024]{1,0:T(8,128)(2,1)S(1)}, bf16[128,1024]{1,0:T(8,128)(2,1)}, u32[]{:S(2)}) copy-start(bf16[128,1024]{1,0:T(8,128)(2,1)} %get-tuple-element.10) | copy-start | bytes 786436
  98.9 1.0 %copy-start.1 = (bf16[128,1024]{1,0:T(8,128)(2,1)S(1)}, bf16[128,1024]{1,0:T(8,128)(2,1)}, u32[]{:S(2)}) copy-start(bf16[128,1024]{1,0:T(8,128)(2,1)} %get-tuple-element.11) | copy-start | bytes 786436

commit v3 on v2

--- a/solution.py
+++ b/solution.py
@@ -205,8 +205,7 @@
         def _():
             @pl.when(n == distance)
             def _():
-                for c in range(2):
-                    hop_in(distance - 1, c).wait_recv()
+                hop_in(distance - 1, 0).wait_recv()
 
             def key_step(t, _):
                 kb = slot * per_block + t
@@ -235,8 +234,10 @@
         return 0
 
     lax.fori_loop(0, distance + 1, score_slot, 0)
-    for pair in g_swap:
-        settle(pair)
+
+    @pl.when(block - distance >= 0)
+    def _():
+        hop_in(distance - 1, 1).wait_recv()
 
     def forward_tile(i, _):
         here = tile_rows(i)
@@ -265,16 +266,45 @@
             inverse = 1.0 / jnp.sum(total[span, :], 1, keepdims=True)
             inv[i, span, :] = jnp.broadcast_to(inverse, (TILE, HD))
             out = made[span, :] * inverse
-            shift = jnp.sum(out * go[i, span, :].astype(jnp.float32), 1, keepdims=True)
-            delta[i, span, :] = jnp.broadcast_to(shift, (TILE, HD))
+            delta[i, span, :] = out
             att[here, cols[h]] = out.astype(jnp.bfloat16)
             qt[i, :, span] = qo[i, span, :].T
-            gt[i, :, span] = go[i, span, :].T
         tile_out(out_at, i, att, q_cols, ao_ref)
         return 0
 
     lax.fori_loop(0, per_block, forward_tile, 0)
 
+    for pair in g_swap:
+        settle(pair)
+
+    def shift_tile(i, _):
+        for h in range(share):
+            span = spans[h]
+            grads = go[i, span, :]
+            shift = jnp.sum(delta[i, span, :] * grads.astype(jnp.float32), 1, keepdims=True)
+            delta[i, span, :] = jnp.broadcast_to(shift, (TILE, HD))
+            gt[i, :, span] = grads.T
+        return 0
+
+    lax.fori_loop(0, per_block, shift_tile, 0)
+
+    def back_tile(slot, t, i):
+        kb = slot * per_block + t
+        keys = band[slot, 0, tile_rows(t), :]
+        values = band[slot, 1, tile_rows(t), :]
+        for h in range(share):
+            span = spans[h]
+            w = kept[i, kb - i, span, :] * twice(inv[i, span, :])
+            dp = across(go[i, span, :], values)
+            wide[0, span, :] = w.astype(jnp.bfloat16)
+            wide[1, span, :] = (w * (dp - twice(delta[i, span, :]))).astype(jnp.bfloat16)
+        for h in range(share):
+            dqs[i, spans[h], :] += jnp.dot(
+                wide[1, spans[h], :], keys, preferred_element_type=jnp.float32
+            )
+        acc[0, kb] += jnp.dot(qt[i], wide[1], preferred_element_type=jnp.float32)
+        acc[1, kb] += jnp.dot(gt[i], wide[0], preferred_element_type=jnp.float32)
+
     def back_slot(slot, _):
         @pl.when(block - (distance - slot) >= 0)
         def _():
@@ -282,40 +312,57 @@
                 kb = slot * per_block + t
 
                 def row_step(i, _):
-                    keys = band[slot, 0, tile_rows(t), :]
-                    values = band[slot, 1, tile_rows(t), :]
-                    for h in range(share):
-                        span = spans[h]
-                        w = kept[i, kb - i, span, :] * twice(inv[i, span, :])
-                        dp = across(go[i, span, :], values)
-                        wide[0, span, :] = w.astype(jnp.bfloat16)
-                        wide[1, span, :] = (w * (dp - twice(delta[i, span, :]))).astype(jnp.bfloat16)
-                    for h in range(share):
-                        dqs[i, spans[h], :] += jnp.dot(
-                            wide[1, spans[h], :], keys, preferred_element_type=jnp.float32
-                        )
-                    acc[0, kb] += jnp.dot(qt[i], wide[1], preferred_element_type=jnp.float32)
-                    acc[1, kb] += jnp.dot(gt[i], wide[0], preferred_element_type=jnp.float32)
+                    back_tile(slot, t, i)
                     return 0
 
-                lax.fori_loop(
-                    jnp.maximum(kb - reach + 1, 0), jnp.minimum(kb + 1, per_block), row_step, 0
-                )
-
-                @pl.when(slot < distance)
+                lax.fori_loop(0, jnp.minimum(kb + 1, per_block), row_step, 0)
+                send_term(slot, t)
+                return 0
+
+            lax.fori_loop(0, per_block, key_step, 0)
+
+        return 0
+
+    strides = min(per_block, 2)
+    near = distance - 1
+
+    def back_rows(first, _):
+        @pl.when(has_prev)
+        def _():
+            def key_step(t, _):
+                def row_step(j, _):
+                    i = j * strides + first
+
+                    @pl.when(i <= near * per_block + t)
+                    def _():
+                        back_tile(near, t, i)
+
+                    return 0
+
+                lax.fori_loop(0, per_block // strides, row_step, 0)
+
+                @pl.when(first == strides - 1)
                 def _():
-                    send_term(slot, t)
-
-                @pl.when(slot == distance)
-                def _():
-                    for h in range(share):
-                        dq[tile_rows(t), cols[h]] = (dqs[t, spans[h], :] * scale).astype(jnp.bfloat16)
-                    tile_out(out_at + 1, t, dq, q_cols, do_ref)
+                    send_term(near, t)
 
                 return 0
 
             lax.fori_loop(0, per_block, key_step, 0)
 
+        def own_rows(j, _):
+            i = (per_block // strides - 1 - j) * strides + first
+
+            def own_step(t, _):
+                back_tile(distance, t, i)
+                return 0
+
+            lax.fori_loop(0, i + 1, own_step, 0)
+            for h in range(share):
+                dq[tile_rows(i), cols[h]] = (dqs[i, spans[h], :] * scale).astype(jnp.bfloat16)
+            tile_out(out_at + 1, i, dq, q_cols, do_ref)
+            return 0
+
+        lax.fori_loop(0, per_block // strides, own_rows, 0)
         return 0
 
     def close_term(slot, c, t):
@@ -338,7 +385,8 @@
         for c in range(2):
             hop_out(slot, c, t).start()
 
-    lax.fori_loop(0, distance + 1, back_slot, 0)
+    lax.fori_loop(0, distance - 1, back_slot, 0)
+    lax.fori_loop(0, strides, back_rows, 0)
 
     def finish(t, _):
         for c in range(2):
@@ -365,6 +413,19 @@
             def _():
                 for t in range(per_block):
                     hop_out(step, c, t).wait_send()
+
+
+def pass_kernel(*refs):
+    ins, outs, held, (in_sem, out_sem) = refs[:4], refs[4:8], refs[8:12], refs[12:]
+    loads = [pltpu.make_async_copy(ins[n], held[n], in_sem.at[n]) for n in range(4)]
+    stores = [pltpu.make_async_copy(held[n], outs[n], out_sem.at[n]) for n in range(4)]
+    for load in loads:
+        load.start()
+    for load, store in zip(loads, stores):
+        load.wait()
+        store.start()
+    for store in stores:
+        store.wait()
 
 
 def per_device(queries, keys, values, grad_out, doc_ids):
@@ -385,7 +446,7 @@
     span = share * TILE
     all_tiles = (distance + 1) * tiles
     swaps = 2 + 2 * share + 4
-    return pl.pallas_call(
+    outs = pl.pallas_call(
         functools.partial(fused_kernel, heads, ctx_low, blocks, distance, HD ** -0.5),
         out_shape=(
             jax.ShapeDtypeStruct(queries.shape, bf16),
@@ -424,6 +485,14 @@
         ),
         name="fused",
     )(doc_ids.reshape(-1, 1, TILE), queries, keys, values, grad_out)
+    return pl.pallas_call(
+        pass_kernel,
+        out_shape=tuple(jax.ShapeDtypeStruct(o.shape, o.dtype) for o in outs),
+        in_specs=[hbm] * 4,
+        out_specs=(hbm,) * 4,
+        scratch_shapes=[pltpu.VMEM(o.shape, o.dtype) for o in outs] + [dma((4,)), dma((4,))],
+        name="hand_on",
+    )(*outs)
 
 
 def solution(mesh):

time: 101 us -> 91.6 us (0.907); the launches traced: 101 us -> 89.8 us
  Pallas kernels: 94.7 us -> 89.2 us
  local copies, waits for them, and re-layouts: 5.22 us -> 0 us
    pallas_call x1, Pallas kernels: 94.7 us -> 86.4 us  [per_device(): pl.pallas_call(functools.partial(fused_kernel, heads, ctx_low, blocks, di...]
    unnamed x10 -> x0, local copies, waits for them, and re-layouts: 5.22 us -> none
    pallas_call x0 -> x1, Pallas kernels: none -> 2.77 us  [per_device(): pl.pallas_call(pass_kernel, out_shape=tuple((jax.ShapeDtypeStruct(o.shape...]
where the time goes in v3:
time: 91.6 us; the launch traced here: 89.8 us
  Pallas kernels  89.2 us (97%)
    pallas_call x1, Pallas kernels, per_device(): pl.pallas_call(functools.partial(fused_kernel, heads, ctx_low, blocks, di...  86.4 us
    pallas_call x1, Pallas kernels, per_device(): pl.pallas_call(pass_kernel, out_shape=tuple((jax.ShapeDtypeStruct(o.shape...  2.77 us

profile of v3, /device:TPU:21, one launch (start us, length us, event | category | flops | bytes accessed | tf_op | source)
XLA Modules:
  0.0 89.8 jit_solution(10279588392583141926)
XLA Ops:
  0.6 86.4 %fused.1 = (bf16[128,4096]{1,0:T(8,128)(2,1)}, bf16[128,4096]{1,0:T(8,128)(2,1)}, bf16[128,1024]{1,0:T(8,128)(2,1)}, bf16[128,1024]{1,0:T(8,128)(2,1)}) custom-call(s32[16,1,256]{2,1,0:T(1,128)} %bitcast.1, bf16[128,4096]{1,0:T(8,128)(2,1)} %q_in.1, bf16[128,1024]{1,0:T(8,128)(2,1)} %k_in.1, bf16[128,1024]{1,0:T(8,128)(2,1)} %v_in.1, bf16[128,4096]{1,0:T(8,128)(2,1)} %g_in.1), custom_call_target="tpu_custom_call" | custom-call | tf_op jit(solution)/shard_map/fused/pallas_call | solution.py:449
  87.0 2.8 %hand_on.1 = (bf16[128,4096]{1,0:T(8,128)(2,1)}, bf16[128,4096]{1,0:T(8,128)(2,1)}, bf16[128,1024]{1,0:T(8,128)(2,1)}, bf16[128,1024]{1,0:T(8,128)(2,1)}) custom-call(bf16[128,4096]{1,0:T(8,128)(2,1)} %get-tuple-element.8.refs_0_, bf16[128,4096]{1,0:T(8,128)(2,1)} %get-tuple-element.9.refs_1_, bf16[128,1024]{1,0:T(8,128)(2,1)} %get-tuple-element.10.refs_2_, ...), custom_call_target="tpu_custom_call" | custom-call | tf_op jit(solution)/shard_map/hand_on/pallas_call | solution.py:488

commit v4 on v3

--- a/solution.py
+++ b/solution.py
@@ -157,10 +157,6 @@
     q_swap = [
         swap_in(2 + h, q_in, h * HD, q_cols, qo.at[my_tile, head_rows(h)]) for h in range(share)
     ]
-    g_swap = [
-        swap_in(2 + share + h, g_in, h * HD, q_cols, go.at[my_tile, head_rows(h)])
-        for h in range(share)
-    ]
     out_at = 2 + 2 * share
     acc[...] = jnp.zeros_like(acc)
     dqs[...] = jnp.zeros_like(dqs)
@@ -186,6 +182,10 @@
 
     for pair in q_swap:
         settle(pair)
+    g_swap = [
+        swap_in(2 + share + h, g_in, h * HD, q_cols, go.at[my_tile, head_rows(h)])
+        for h in range(share)
+    ]
 
     spans = [slice(h * TILE, (h + 1) * TILE) for h in range(share)]
     cols = [slice(h * HD, (h + 1) * HD) for h in range(share)]
@@ -280,13 +280,40 @@
     def shift_tile(i, _):
         for h in range(share):
             span = spans[h]
-            grads = go[i, span, :]
-            shift = jnp.sum(delta[i, span, :] * grads.astype(jnp.float32), 1, keepdims=True)
-            delta[i, span, :] = jnp.broadcast_to(shift, (TILE, HD))
+            grads = go[i, span, :].astype(jnp.float32)
+            shift = jnp.sum(delta[i, span, :] * grads, 1, keepdims=True)
+            shares = inv[i, span, :]
+            delta[i, span, :] = shift * shares
+            grads = (grads * shares).astype(jnp.bfloat16)
+            go[i, span, :] = grads
             gt[i, :, span] = grads.T
         return 0
 
     lax.fori_loop(0, per_block, shift_tile, 0)
+
+    def back_both(slot, t, one, two):
+        kb = slot * per_block + t
+        keys = band[slot, 0, tile_rows(t), :]
+        values = band[slot, 1, tile_rows(t), :]
+        for n, i in enumerate((one, two)):
+            for h in range(share):
+                span = spans[h]
+                w = kept[i, kb - i, span, :]
+                dp = across(go[i, span, :], values)
+                wide[2 * n, span, :] = w.astype(jnp.bfloat16)
+                grown = w * (dp - twice(delta[i, span, :]))
+                wide[2 * n + 1, span, :] = grown.astype(jnp.bfloat16)
+        for n, i in enumerate((one, two)):
+            for h in range(share):
+                dqs[i, spans[h], :] += jnp.dot(
+                    wide[2 * n + 1, spans[h], :], keys, preferred_element_type=jnp.float32
+                )
+        acc[0, kb] += jnp.dot(qt[one], wide[1], preferred_element_type=jnp.float32) + jnp.dot(
+            qt[two], wide[3], preferred_element_type=jnp.float32
+        )
+        acc[1, kb] += jnp.dot(gt[one], wide[0], preferred_element_type=jnp.float32) + jnp.dot(
+            gt[two], wide[2], preferred_element_type=jnp.float32
+        )
 
     def back_tile(slot, t, i):
         kb = slot * per_block + t
@@ -294,7 +321,7 @@
         values = band[slot, 1, tile_rows(t), :]
         for h in range(share):
             span = spans[h]
-            w = kept[i, kb - i, span, :] * twice(inv[i, span, :])
+            w = kept[i, kb - i, span, :]
             dp = across(go[i, span, :], values)
             wide[0, span, :] = w.astype(jnp.bfloat16)
             wide[1, span, :] = (w * (dp - twice(delta[i, span, :]))).astype(jnp.bfloat16)
@@ -311,11 +338,19 @@
             def key_step(t, _):
                 kb = slot * per_block + t
 
-                def row_step(i, _):
-                    back_tile(slot, t, i)
+                count = jnp.minimum(kb + 1, per_block)
+
+                def row_step(j, _):
+                    back_both(slot, t, 2 * j, 2 * j + 1)
                     return 0
 
-                lax.fori_loop(0, jnp.minimum(kb + 1, per_block), row_step, 0)
+                if per_block > 1:
+                    lax.fori_loop(0, count // 2, row_step, 0)
+
+                @pl.when(lax.rem(count, 2) == 1)
+                def _():
+                    back_tile(slot, t, count - 1)
+
                 send_term(slot, t)
                 return 0
 
@@ -330,16 +365,24 @@
         @pl.when(has_prev)
         def _():
             def key_step(t, _):
-                def row_step(j, _):
-                    i = j * strides + first
-
-                    @pl.when(i <= near * per_block + t)
+                kb = near * per_block + t
+                if strides * 2 == per_block:
+                    @pl.when(strides + first <= kb)
                     def _():
-                        back_tile(near, t, i)
-
-                    return 0
-
-                lax.fori_loop(0, per_block // strides, row_step, 0)
+                        back_both(near, t, first, strides + first)
+
+                    @pl.when((first <= kb) & (strides + first > kb))
+                    def _():
+                        back_tile(near, t, first)
+                else:
+                    def row_step(j, _):
+                        @pl.when(j * strides + first <= kb)
+                        def _():
+                            back_tile(near, t, j * strides + first)
+
+                        return 0
+
+                    lax.fori_loop(0, per_block // strides, row_step, 0)
 
                 @pl.when(first == strides - 1)
                 def _():
@@ -349,20 +392,35 @@
 
             lax.fori_loop(0, per_block, key_step, 0)
 
-        def own_rows(j, _):
-            i = (per_block // strides - 1 - j) * strides + first
-
-            def own_step(t, _):
-                back_tile(distance, t, i)
-                return 0
-
-            lax.fori_loop(0, i + 1, own_step, 0)
-            for h in range(share):
-                dq[tile_rows(i), cols[h]] = (dqs[i, spans[h], :] * scale).astype(jnp.bfloat16)
-            tile_out(out_at + 1, i, dq, q_cols, do_ref)
+        def own_step(t, _):
+            if strides * 2 == per_block:
+                @pl.when(t <= first)
+                def _():
+                    back_both(distance, t, first, strides + first)
+
+                @pl.when((t > first) & (t <= strides + first))
+                def _():
+                    back_tile(distance, t, strides + first)
+            else:
+                def row_step(j, _):
+                    @pl.when(t <= j * strides + first)
+                    def _():
+                        back_tile(distance, t, j * strides + first)
+
+                    return 0
+
+                lax.fori_loop(0, per_block // strides, row_step, 0)
+
+            @pl.when(lax.rem(t, strides) == first)
+            def _():
+                for h in range(share):
+                    grown = dqs[t, spans[h], :] * scale
+                    dq[tile_rows(t), cols[h]] = grown.astype(jnp.bfloat16)
+                tile_out(out_at + 1, t, dq, q_cols, do_ref)
+
             return 0
 
-        lax.fori_loop(0, per_block // strides, own_rows, 0)
+        lax.fori_loop(0, per_block, own_step, 0)
         return 0
 
     def close_term(slot, c, t):
@@ -474,7 +532,7 @@
             pltpu.VMEM((tokens, share * HD), bf16),
             pltpu.VMEM((distance + 1, 2, tokens, HD), bf16),
             pltpu.VMEM((distance, 2, tokens, HD), bf16),
-            pltpu.VMEM((2, span, TILE), bf16),
+            pltpu.VMEM((4, span, TILE), bf16),
             pltpu.VMEM((tiles, TILE, HD), jnp.int32),
             dma((swaps,)), dma((swaps, group - 1)), dma((swaps, group - 1)),
             dma((distance, 2)), dma((distance, 2)),

time: 91.6 us -> 87 us (0.950); the launches traced: 89.8 us -> 86.7 us
  Pallas kernels: 89.2 us -> 86 us
    pallas_call x1, Pallas kernels: 86.4 us -> 83.3 us  [per_device(): pl.pallas_call(functools.partial(fused_kernel, heads, ctx_low, blocks, di...]
where the time goes in v4:
time: 87 us; the launch traced here: 86.7 us
  Pallas kernels  86 us (99%)
    pallas_call x1, Pallas kernels, per_device(): pl.pallas_call(functools.partial(fused_kernel, heads, ctx_low, blocks, di...  83.3 us
    pallas_call x1, Pallas kernels, per_device(): pl.pallas_call(pass_kernel, out_shape=tuple((jax.ShapeDtypeStruct(o.shape...  2.77 us

profile of v4, /device:TPU:21, one launch (start us, length us, event | category | flops | bytes accessed | tf_op | source)
XLA Modules:
  0.0 86.7 jit_solution(57145838305964421)
XLA Ops:
  0.6 83.3 %fused.1 = (bf16[128,4096]{1,0:T(8,128)(2,1)}, bf16[128,4096]{1,0:T(8,128)(2,1)}, bf16[128,1024]{1,0:T(8,128)(2,1)}, bf16[128,1024]{1,0:T(8,128)(2,1)}) custom-call(s32[16,1,256]{2,1,0:T(1,128)} %bitcast.1, bf16[128,4096]{1,0:T(8,128)(2,1)} %q_in.1, bf16[128,1024]{1,0:T(8,128)(2,1)} %k_in.1, bf16[128,1024]{1,0:T(8,128)(2,1)} %v_in.1, bf16[128,4096]{1,0:T(8,128)(2,1)} %g_in.1), custom_call_target="tpu_custom_call" | custom-call | tf_op jit(solution)/shard_map/fused/pallas_call | solution.py:507
  83.9 2.8 %hand_on.1 = (bf16[128,4096]{1,0:T(8,128)(2,1)}, bf16[128,4096]{1,0:T(8,128)(2,1)}, bf16[128,1024]{1,0:T(8,128)(2,1)}, bf16[128,1024]{1,0:T(8,128)(2,1)}) custom-call(bf16[128,4096]{1,0:T(8,128)(2,1)} %get-tuple-element.8.refs_0_, bf16[128,4096]{1,0:T(8,128)(2,1)} %get-tuple-element.9.refs_1_, bf16[128,1024]{1,0:T(8,128)(2,1)} %get-tuple-element.10.refs_2_, ...), custom_call_target="tpu_custom_call" | custom-call | tf_op jit(solution)/shard_map/hand_on/pallas_call | solution.py:546

commit v5 on v4

--- a/solution.py
+++ b/solution.py
@@ -247,20 +247,35 @@
         total[...] = jnp.zeros_like(total)
         made[...] = jnp.zeros_like(made)
 
-        def forward(kb, _):
+        def part(kb, h):
             slot = kb // per_block
             values = band[slot, 1, tile_rows(kb - slot * per_block), :]
+            span = spans[h]
+            p = jnp.exp2(kept[i, kb - i, span, :] * factor - twice(peak[i, span, :]))
+            kept[i, kb - i, span, :] = p
+            grown = jnp.dot(p.astype(jnp.bfloat16), values, preferred_element_type=jnp.float32)
+            return p[:, :HD] + p[:, HD:], grown
+
+        def forward(n, _):
+            kb = i + reach - 2 - 2 * n
             for h in range(share):
-                span = spans[h]
-                p = jnp.exp2(kept[i, kb - i, span, :] * factor - twice(peak[i, span, :]))
-                kept[i, kb - i, span, :] = p
-                total[span, :] += p[:, :HD] + p[:, HD:]
-                made[span, :] += jnp.dot(
-                    p.astype(jnp.bfloat16), values, preferred_element_type=jnp.float32
-                )
+                sum_a, grown_a = part(kb, h)
+                sum_b, grown_b = part(kb + 1, h)
+                total[spans[h], :] += sum_a + sum_b
+                made[spans[h], :] += grown_a + grown_b
             return 0
 
-        lax.fori_loop(jnp.maximum(i, first_kb), i + reach, forward, 0)
+        lowest = jnp.maximum(i, first_kb)
+        count = i + reach - lowest
+
+        @pl.when(lax.rem(count, 2) == 1)
+        def _():
+            for h in range(share):
+                sum_a, grown_a = part(lowest, h)
+                total[spans[h], :] += sum_a
+                made[spans[h], :] += grown_a
+
+        lax.fori_loop(0, count // 2, forward, 0)
         for h in range(share):
             span = spans[h]
             inverse = 1.0 / jnp.sum(total[span, :], 1, keepdims=True)

time: 87 us -> 86.7 us (level)
  no operation moved by 1% of the time
where the time goes in v5:
time: 86.7 us; the launch traced here: 86.5 us
  Pallas kernels  85.8 us (99%)
    pallas_call x1, Pallas kernels, per_device(): pl.pallas_call(functools.partial(fused_kernel, heads, ctx_low, blocks, di...  83.1 us
    pallas_call x1, Pallas kernels, per_device(): pl.pallas_call(pass_kernel, out_shape=tuple((jax.ShapeDtypeStruct(o.shape...  2.77 us

profile of v5, /device:TPU:21, one launch (start us, length us, event | category | flops | bytes accessed | tf_op | source)
XLA Modules:
  0.0 86.5 jit_solution(17548660194194723609)
XLA Ops:
  0.6 83.1 %fused.1 = (bf16[128,4096]{1,0:T(8,128)(2,1)}, bf16[128,4096]{1,0:T(8,128)(2,1)}, bf16[128,1024]{1,0:T(8,128)(2,1)}, bf16[128,1024]{1,0:T(8,128)(2,1)}) custom-call(s32[16,1,256]{2,1,0:T(1,128)} %bitcast.1, bf16[128,4096]{1,0:T(8,128)(2,1)} %q_in.1, bf16[128,1024]{1,0:T(8,128)(2,1)} %k_in.1, bf16[128,1024]{1,0:T(8,128)(2,1)} %v_in.1, bf16[128,4096]{1,0:T(8,128)(2,1)} %g_in.1), custom_call_target="tpu_custom_call" | custom-call | tf_op jit(solution)/shard_map/fused/pallas_call | solution.py:522
  83.7 2.8 %hand_on.1 = (bf16[128,4096]{1,0:T(8,128)(2,1)}, bf16[128,4096]{1,0:T(8,128)(2,1)}, bf16[128,1024]{1,0:T(8,128)(2,1)}, bf16[128,1024]{1,0:T(8,128)(2,1)}) custom-call(bf16[128,4096]{1,0:T(8,128)(2,1)} %get-tuple-element.8.refs_0_, bf16[128,4096]{1,0:T(8,128)(2,1)} %get-tuple-element.9.refs_1_, bf16[128,1024]{1,0:T(8,128)(2,1)} %get-tuple-element.10.refs_2_, ...), custom_call_target="tpu_custom_call" | custom-call | tf_op jit(solution)/shard_map/hand_on/pallas_call | solution.py:561
